TPU v7x, 256 devices: a whole 4x4x8 slice. The times are simulated.
256 devices in a mesh: dom: 32 (over y, z), feat: 8 (over x, core).
Axes of the slice: x: 4, y: 4, z: 8, core: 2. Of those that a mesh axis runs over, the one named last changes fastest.
Arguments:
- feats: bfloat16 [131072, 1024], P('dom', 'feat'), may hold values from -6 to 6
- projection: bfloat16 [1024, 512], P('feat'), may hold values from -0.1875 to 0.1875
- tiles: bfloat16 [8192, 4, 128, 128], P(('dom', 'feat')), may hold values from -0.25 to 0.25
- slot_owner: int32 [8192, 1], P(('dom', 'feat')), may hold values from 0 to 31; in each aligned block of 32 rows (0 to 31, 32 to 63, ...) at most 2 rows name the same one
- slot_block: int32 [8192, 1], P(('dom', 'feat')), may hold values from 0 to 3
- source_block: int32 [8192, 4], P(('dom', 'feat')), may hold values from 0 to 3
- counts: int32 [131072], P(('dom', 'feat')), may hold values from 1 to 4
- out_grad: bfloat16 [131072, 256], P(('dom', 'feat')), may hold values from -0.015625 to 0.015625
Outputs:
- activated: bfloat16 [131072, 256], P(('dom', 'feat'))
- weight_grad: float32 [1024, 512], P('feat')
Inputs may be any that keep to these rules, and one draw needn't show every extreme that they name: `slot_owner`: among the 32 sent rows of one device, no dom index is named more than 2 times; some device names one exactly 2 times.
All inputs are finite; a program needn't handle non-finite values.
Results may differ from a plain program's by a relative error of at most 0.0059.
Values may be sent and summed in bfloat16 or wider, within the bound.
A program may use at most 128 MiB of HBM per device.

v0:
```python
import jax
import jax.numpy as jnp
from jax import lax
from jax.sharding import PartitionSpec as P


def local(feats, projection, tiles, slot_owner, slot_block, source_block, counts, out_grad):
    tile_size = tiles.shape[-1]
    slot_count = tiles.shape[0]
    per_slot = tiles.shape[1]
    out_width = out_grad.shape[1]
    node_rows = out_grad.shape[0]
    block_count = node_rows // tile_size
    dom_count = lax.axis_size("dom")
    capacity = max(2, 2 * slot_count // dom_count)
    flat_width = tile_size * out_width
    projected = lax.psum_scatter(
        jnp.dot(feats, projection, preferred_element_type=jnp.float32),
        "feat",
        scatter_dimension=0,
        tiled=True,
    ).astype(jnp.bfloat16)
    neighbour = projected[:, :out_width].reshape(block_count, tile_size, out_width)
    self_part = projected[:, out_width:]
    picked = neighbour[source_block]
    contribution = jnp.einsum("skij,skjh->sih", tiles, picked, preferred_element_type=jnp.float32)
    contribution = contribution.astype(jnp.bfloat16).reshape(slot_count, flat_width)
    slot_dest = slot_owner[:, 0]
    dest_block = slot_block[:, 0]
    dest_hot = (slot_dest[:, None] == jnp.arange(dom_count, dtype=jnp.int32)[None, :]).astype(
        jnp.int32
    )
    before = jnp.cumsum(dest_hot, axis=0) - dest_hot
    position = jnp.sum(before * dest_hot, axis=1)
    slot_index = slot_dest * capacity + position
    placing = jnp.arange(dom_count * capacity, dtype=jnp.int32)[:, None] == slot_index[None, :]
    outgoing = jnp.dot(
        placing.astype(jnp.bfloat16), contribution, preferred_element_type=jnp.float32
    )
    outgoing = outgoing.astype(jnp.bfloat16).reshape(dom_count, capacity, flat_width)
    labels = jnp.sum(placing.astype(jnp.int32) * (dest_block + 1)[None, :], axis=1) - 1
    labels = labels.reshape(dom_count, capacity)
    incoming, got_labels = (
        lax.all_to_all(outgoing, "dom", split_axis=0, concat_axis=0, tiled=True),
        lax.all_to_all(labels, "dom", split_axis=0, concat_axis=0, tiled=True),
    )
    incoming = incoming.reshape(dom_count * capacity, flat_width)
    receive_hot = (
        jnp.arange(block_count, dtype=jnp.int32)[:, None] == got_labels.reshape(-1)[None, :]
    ).astype(jnp.bfloat16)
    summed = jnp.dot(receive_hot, incoming, preferred_element_type=jnp.float32).reshape(
        node_rows, out_width
    )
    degree = counts.astype(jnp.float32)[:, None]
    preact = summed / degree + self_part.astype(jnp.float32)
    sigma = jax.nn.sigmoid(preact)
    activated = (preact * sigma).astype(jnp.bfloat16)
    grad_pre = out_grad.astype(jnp.float32) * sigma * (1.0 + preact * (1.0 - sigma))
    grad_self = grad_pre.astype(jnp.bfloat16)
    grad_sum = (grad_pre / degree).astype(jnp.bfloat16).reshape(block_count, flat_width)
    sending_back = jnp.dot(receive_hot.T, grad_sum, preferred_element_type=jnp.float32)
    sending_back = sending_back.astype(jnp.bfloat16).reshape(dom_count, capacity, flat_width)
    returned = lax.all_to_all(sending_back, "dom", split_axis=0, concat_axis=0, tiled=True).reshape(
        dom_count * capacity, flat_width
    )
    slot_grad = jnp.dot(
        placing.T.astype(jnp.bfloat16), returned, preferred_element_type=jnp.float32
    )
    slot_grad = slot_grad.astype(jnp.bfloat16).reshape(slot_count, tile_size, out_width)
    products = jnp.einsum("skij,sih->skjh", tiles, slot_grad, preferred_element_type=jnp.float32)
    source_hot = (
        jnp.arange(block_count, dtype=jnp.int32)[:, None] == source_block.reshape(-1)[None, :]
    ).astype(jnp.float32)
    flat_products = products.reshape(slot_count * per_slot, tile_size, out_width)
    grad_neigh = jnp.einsum(
        "bn,njh->bjh", source_hot, flat_products, precision=lax.Precision.HIGHEST
    )
    grad_neigh = grad_neigh.astype(jnp.bfloat16).reshape(node_rows, out_width)
    grad_proj = jnp.concatenate([grad_neigh, grad_self], axis=1)
    partial_grad = lax.dot_general(
        feats,
        lax.all_gather(grad_proj, "feat", axis=0, tiled=True),
        (((0,), (0,)), ((), ())),
        preferred_element_type=jnp.float32,
    )
    weight_grad = lax.psum(partial_grad, "dom")
    return (activated, weight_grad)


def solution(mesh):
    placed = (
        P("dom", "feat"),
        P("feat", None),
        P(("dom", "feat"), None, None, None),
        P(("dom", "feat"), None),
        P(("dom", "feat"), None),
        P(("dom", "feat"), None),
        P(("dom", "feat")),
        P(("dom", "feat"), None),
    )
    return jax.shard_map(
        local,
        mesh=mesh,
        in_specs=placed,
        out_specs=(P(("dom", "feat"), None), P("feat", None)),
        check_vma=False,
    )
```

profile of v0, /device:TPU:2, one launch (start us, length us, event | category | flops | bytes accessed | tf_op | source)
XLA Modules:
  0.0 570.8 jit_solution(17779581834681642743)
XLA Ops:
  8.4 5.4 fusion.12
  15.6 11.5 %all-to-all-start = ((s32[32,1,2]{2,1,0:T(1,128)}), s32[32,1,2]{2,1,0:T(1,128)S(1)}, u32[]{:S(2)}, u32[]{:S(2)}) async-start(s32[32,1,2]{2,1,0:T(1,128)} %bitcast.2), calls=%async_computation | async-start | bytes 32768 | tf_op jit(solution)/shard_map/all_to_all | solution.py:45
  27.3 42.2 %reduce-scatter.2.cloned.1.call-done = f32[512,512]{1,0:T(8,128)} async-done(((f32[4096,512]{1,0:T(8,128)}), f32[512,512]{1,0:T(8,128)}) %reduce-scatter.2.cloned.1.call-update) | async-done | bytes 1048592 | tf_op jit(solution)/shard_map/reduce_scatter | solution.py:17
  71.7 6.5 %gather_fusion = bf16[128,128,256]{2,1,0:T(8,128)(2,1)} fusion(bf16[4,128,256]{2,1,0:T(8,128)(2,1)S(1)} %bitcast.46, s32[1024]{0:T(1024)S(1)} %pad_clamp_fusion), kind=kCustom, calls=%fused_computation | custom fusion | bytes 16777728 | tf_op jit(solution)/shard_map/gather | solution.py:25
  78.2 7.0 %fusion.2 = bf16[32,128,256]{1,2,0:T(8,128)(2,1)S(1)} fusion(bf16[32,4,128,256]{3,2,1,0:T(8,128)(2,1)} %bitcast.48, bf16[32,4,128,128]{3,2,1,0:T(8,128)(2,1)} %param.10), kind=kOutput, calls=%fused_computation.7 | convolution fusion | flops 1074790400 | bytes 14680064 | tf_op jit(solution)/shard_map/skij,skjh->sih/dot_general | solution.py:26
  85.2 2.9 copy.47
  88.1 4.9 convolution_convert_fusion.1
  93.0 7.6 %reshape.74 = bf16[32,2,32768]{2,1,0:T(2,128)(2,1)} reshape(bf16[64,32768]{1,0:T(8,128)(2,1)} %convolution_convert_fusion.1) | data formatting | bytes 8388608 | tf_op jit(solution)/shard_map/reshape | solution.py:40
  100.6 10.5 %all-to-all-start.1 = ((bf16[32,2,32768]{2,1,0:T(2,128)(2,1)}), bf16[32,2,32768]{2,1,0:T(2,128)(2,1)}, u32[]{:S(2)}, u32[]{:S(2)}) async-start(bf16[32,2,32768]{2,1,0:T(2,128)(2,1)} %reshape.74), calls=%async_computation.2 | async-start | bytes 8388608 | tf_op jit(solution)/shard_map/all_to_all | solution.py:44
  112.5 96.4 %all-to-all-done.1 = bf16[32,2,32768]{2,1,0:T(2,128)(2,1)} async-done(((bf16[32,2,32768]{2,1,0:T(2,128)(2,1)}), bf16[32,2,32768]{2,1,0:T(2,128)(2,1)}, u32[]{:S(2)}, u32[]{:S(2)}) %all-to-all-start.1) | async-done | bytes 4194336 | tf_op jit(solution)/shard_map/all_to_all | solution.py:44
  208.9 7.3 %reshape.75 = bf16[64,32768]{1,0:T(8,128)(2,1)} reshape(bf16[32,2,32768]{2,1,0:T(2,128)(2,1)} %all-to-all-done.1) | data formatting | bytes 8388608 | tf_op jit(solution)/shard_map/reshape | solution.py:47
  216.2 2.9 fusion.6
  220.8 3.2 convolution_convert_fusion
  224.0 7.6 %reshape.78 = bf16[32,2,32768]{2,1,0:T(2,128)(2,1)} reshape(bf16[64,32768]{1,0:T(8,128)(2,1)} %convolution_convert_fusion) | data formatting | bytes 8388608 | tf_op jit(solution)/shard_map/reshape | solution.py:62
  231.7 8.5 %all-to-all-start.2 = ((bf16[32,2,32768]{2,1,0:T(2,128)(2,1)}), bf16[32,2,32768]{2,1,0:T(2,128)(2,1)}, u32[]{:S(2)}, u32[]{:S(2)}) async-start(bf16[32,2,32768]{2,1,0:T(2,128)(2,1)} %reshape.78), calls=%async_computation.3 | async-start | bytes 8388608 | tf_op jit(solution)/shard_map/all_to_all | solution.py:63
  240.4 95.7 %all-to-all-done.2 = bf16[32,2,32768]{2,1,0:T(2,128)(2,1)} async-done(((bf16[32,2,32768]{2,1,0:T(2,128)(2,1)}), bf16[32,2,32768]{2,1,0:T(2,128)(2,1)}, u32[]{:S(2)}, u32[]{:S(2)}) %all-to-all-start.2) | async-done | bytes 4194336 | tf_op jit(solution)/shard_map/all_to_all | solution.py:63
  336.1 7.3 %reshape.79 = bf16[64,32768]{1,0:T(8,128)(2,1)} reshape(bf16[32,2,32768]{2,1,0:T(2,128)(2,1)} %all-to-all-done.2) | data formatting | bytes 8388608 | tf_op jit(solution)/shard_map/reshape | solution.py:63
  343.4 3.1 convolution_convert_fusion.2
  347.0 8.1 %fusion = f32[32,256,4,128]{3,1,2,0:T(8,128)} fusion(bf16[32,4,128,128]{3,2,1,0:T(8,128)(2,1)S(1)} %copy-done.1, bf16[32,128,256]{2,1,0:T(8,128)(2,1)S(1)} %bitcast.52), kind=kOutput, calls=%fused_computation.5 | convolution fusion | flops 1073741824 | bytes 23068672 | tf_op jit(solution)/shard_map/skij,sih->skjh/dot_general | solution.py:70
  355.1 17.7 %copy.40 = f32[128,128,256]{2,0,1:T(8,128)} copy(f32[128,128,256]{1,2,0:T(8,128)} %bitcast.47) | data formatting | bytes 33554432 | tf_op jit(solution)/shard_map/reshape | solution.py:74
  372.8 9.0 %convolution_convert_fusion.3 = bf16[4,128,256]{2,0,1:T(4,128)(2,1)S(1)} fusion(f32[128,128,256]{2,0,1:T(8,128)} %copy.40, s32[128]{0:T(128)S(1)} %eq.67), kind=kOutput, calls=%fused_computation.8 | convolution fusion | flops 201458176 | bytes 17039872 | tf_op jit(solution)/shard_map/bn,njh->bjh/dot_general | solution.py:75
  382.7 30.2 %all-gather.2.cloned.1.call-done = bf16[4096,512]{1,0:T(8,128)(2,1)} async-done(((bf16[512,512]{1,0:T(8,128)(2,1)}), bf16[4096,512]{1,0:T(8,128)(2,1)}) %all-gather.2.cloned.1.call-update) | async-done | bytes 4194320 | tf_op jit(solution)/shard_map/all_gather | solution.py:82
  413.0 4.2 convolution_bitcast_fusion
  417.2 145.3 %all-reduce.2.cloned.1.call-done = f32[128,512]{0,1:T(8,128)} async-done(((f32[128,512]{0,1:T(8,128)}), f32[128,512]{0,1:T(8,128)}) %all-reduce.2.cloned.1.call-update) | async-done | bytes 262160 | tf_op jit(solution)/shard_map/psum | solution.py:86
  (52 shorter events, 11.8 us)
Async XLA Ops:
  7.2 1.2 copy-start
  7.2 62.4 %reduce-scatter.2.cloned.1.call-start = ((), (), s32[]{:S(2)}) async-start(), calls=%async_computation.4 | async-start | bytes 9437184 | tf_op jit(solution)/shard_map/reduce_scatter | solution.py:17
  13.8 0.7 copy-start.6
  13.8 1.0 copy-start.8
  13.8 13.3 %copy-start.5 = (s32[32,4]{0,1:T(4,128)S(1)}, s32[32,4]{0,1:T(4,128)}, u32[]{:S(2)}) copy-start(s32[32,4]{0,1:T(4,128)} %param.13) | copy-start | bytes 1540
  15.6 85.1 %all-to-all-start = ((s32[32,1,2]{2,1,0:T(1,128)}), s32[32,1,2]{2,1,0:T(1,128)S(1)}, u32[]{:S(2)}, u32[]{:S(2)}) async-start(s32[32,1,2]{2,1,0:T(1,128)} %bitcast.2), calls=%async_computation | async-start | bytes 32768 | tf_op jit(solution)/shard_map/all_to_all | solution.py:45
  70.8 0.8 copy-start.2
  100.6 10.5 %copy-start.7 = (s32[512]{0:T(512)S(1)}, s32[512]{0:T(512)}, u32[]{:S(2)}) copy-start(s32[512]{0:T(512)} %param.14) | copy-start | bytes 6148
  100.6 108.3 %all-to-all-start.1 = ((bf16[32,2,32768]{2,1,0:T(2,128)(2,1)}), bf16[32,2,32768]{2,1,0:T(2,128)(2,1)}, u32[]{:S(2)}, u32[]{:S(2)}) async-start(bf16[32,2,32768]{2,1,0:T(2,128)(2,1)} %reshape.74), calls=%async_computation.2 | async-start | bytes 8388608 | tf_op jit(solution)/shard_map/all_to_all | solution.py:44
  216.2 3.3 copy-start.3
  216.2 3.3 copy-start.4
  231.7 104.5 %all-to-all-start.2 = ((bf16[32,2,32768]{2,1,0:T(2,128)(2,1)}), bf16[32,2,32768]{2,1,0:T(2,128)(2,1)}, u32[]{:S(2)}, u32[]{:S(2)}) async-start(bf16[32,2,32768]{2,1,0:T(2,128)(2,1)} %reshape.78), calls=%async_computation.3 | async-start | bytes 8388608 | tf_op jit(solution)/shard_map/all_to_all | solution.py:63
  240.2 172.8 %all-gather.2.cloned.1.call-start = ((), (), s32[]{:S(2)}) async-start(), calls=%async_computation.5 | async-start | bytes 4718592 | tf_op jit(solution)/shard_map/all_gather | solution.py:82
  343.4 3.6 copy-start.1
  382.7 179.8 %all-reduce.2.cloned.1.call-start = ((), (), s32[]{:S(2)}) async-start(), calls=%async_computation.6 | async-start | bytes 524288 | tf_op jit(solution)/shard_map/psum | solution.py:86
Sparse Core Ops, SparseCore 0:
  13.9 55.5 reduce-scatter.1
  382.8 30.1 all-gather.1
  417.3 145.1 all-reduce.1
where the time goes:
time: 572 us; the launch traced here: 571 us
  waiting for transfers between devices  410 us (72%)
  local copies, waits for them, and re-layouts  64.1 us (11%)
  matrix products  47.8 us (8%)
  starting transfers between devices  30.6 us (5%)
  between operations  13.9 us (2%)
    psum x1, waiting for transfers between devices, local(): weight_grad = lax.psum(partial_grad, 'dom')  145 us
    all_to_all x1, waiting for transfers between devices, local(): lax.all_to_all(outgoing, 'dom', split_axis=0, concat_axis=0, tiled=True)  96.4 us
    all_to_all x1, waiting for transfers between devices, local(): lax.all_to_all(sending_back, 'dom', split_axis=0, concat_axis=0, tiled=True)  95.7 us
    reduce_scatter x1, waiting for transfers between devices, local(): lax.psum_scatter(jnp.dot(feats, projection, preferred_element_type=jnp.fl...  42.2 us
    all_gather x1, waiting for transfers between devices, local(): lax.all_gather(grad_proj, 'feat', axis=0, tiled=True)  30.2 us
    reshape x1, local copies, waits for them, and re-layouts, local(): products.reshape(slot_count * per_slot, tile_size, out_width)  17.7 us
    all_to_all x1, starting transfers between devices, local(): lax.all_to_all(labels, 'dom', split_axis=0, concat_axis=0, tiled=True)  11.5 us
  transfers between devices with their start and end apart: 6, of which 5 were waited for; matrix products, arithmetic and copies ran while one was open for 6% of the time, Pallas kernels for 0%

commit v1 on v0

--- a/solution.py
+++ b/solution.py
@@ -83,7 +83,11 @@
         (((0,), (0,)), ((), ())),
         preferred_element_type=jnp.float32,
     )
-    weight_grad = lax.psum(partial_grad, "dom")
+    weight_grad = partial_grad
+    for hop in (1, 2, 4, 8, 16):
+        weight_grad = weight_grad + lax.ppermute(
+            weight_grad, "dom", [(dev, dev ^ hop) for dev in range(32)]
+        )
     return (activated, weight_grad)
 
 

time: 572 us -> 484 us (0.85)
  waiting for transfers between devices: 410 us -> 305 us
  starting transfers between devices: 30.6 us -> 46.4 us
    psum x1 -> x0, waiting for transfers between devices: 145 us -> none  [local(): weight_grad = lax.psum(partial_grad, 'dom')]
    ppermute x0 -> x5, waiting for transfers between devices: none -> 40.2 us  [local(): lax.ppermute(weight_grad, 'dom', [(dev, dev ^ hop) for dev in range(32)])]
    ppermute x0 -> x5, starting transfers between devices: none -> 15.8 us  [local(): lax.ppermute(weight_grad, 'dom', [(dev, dev ^ hop) for dev in range(32)])]
  transfers between devices with their start and end apart: 6 -> 10, of which waited for: 5 -> 9; matrix products, arithmetic and copies ran while one was open for 6% -> 7% of each run, Pallas kernels for 0% -> 0%
where the time goes in v1:
time: 484 us; the launch traced here: 480 us
  waiting for transfers between devices  305 us (63%)
  local copies, waits for them, and re-layouts  63.3 us (13%)
  matrix products  47.1 us (10%)
  starting transfers between devices  46.4 us (10%)
  between operations  14.3 us (3%)
    all_to_all x1, waiting for transfers between devices, local(): lax.all_to_all(outgoing, 'dom', split_axis=0, concat_axis=0, tiled=True)  96.4 us
    all_to_all x1, waiting for transfers between devices, local(): lax.all_to_all(sending_back, 'dom', split_axis=0, concat_axis=0, tiled=True)  95.7 us
    reduce_scatter x1, waiting for transfers between devices, local(): lax.psum_scatter(jnp.dot(feats, projection, preferred_element_type=jnp.fl...  42.2 us
    ppermute x5, waiting for transfers between devices, local(): lax.ppermute(weight_grad, 'dom', [(dev, dev ^ hop) for dev in range(32)])  40.2 us
    all_gather x1, waiting for transfers between devices, local(): lax.all_gather(grad_proj, 'feat', axis=0, tiled=True)  30.3 us
    reshape x1, local copies, waits for them, and re-layouts, local(): products.reshape(slot_count * per_slot, tile_size, out_width)  17.7 us
    ppermute x5, starting transfers between devices, local(): lax.ppermute(weight_grad, 'dom', [(dev, dev ^ hop) for dev in range(32)])  15.8 us
    all_to_all x1, starting transfers between devices, local(): lax.all_to_all(labels, 'dom', split_axis=0, concat_axis=0, tiled=True)  11.5 us
  transfers between devices with their start and end apart: 10, of which 9 were waited for; matrix products, arithmetic and copies ran while one was open for 7% of the time, Pallas kernels for 0%

profile of v1, /device:TPU:2, one launch (start us, length us, event | category | flops | bytes accessed | tf_op | source)
XLA Modules:
  0.0 480.4 jit_solution(16887241822676697801)
XLA Ops:
  8.4 5.3 %fusion.12 = f32[4096,512]{1,0:T(8,128)} fusion(bf16[4096,128]{1,0:T(8,128)(2,1)S(1)} %copy-done, bf16[128,512]{1,0:T(8,128)(2,1)} %param.9), kind=kOutput, calls=%fused_computation.35 | convolution fusion | flops 536870912 | bytes 9568256 | tf_op jit(solution)/shard_map/dot_general | solution.py:18
  15.6 11.5 %all-to-all-start = ((s32[32,1,2]{2,1,0:T(1,128)}), s32[32,1,2]{2,1,0:T(1,128)S(1)}, u32[]{:S(2)}, u32[]{:S(2)}) async-start(s32[32,1,2]{2,1,0:T(1,128)} %bitcast.2), calls=%async_computation | async-start | bytes 32768 | tf_op jit(solution)/shard_map/all_to_all | solution.py:45
  27.3 42.2 %reduce-scatter.2.cloned.1.call-done = f32[512,512]{1,0:T(8,128)} async-done(((f32[4096,512]{1,0:T(8,128)}), f32[512,512]{1,0:T(8,128)}) %reduce-scatter.2.cloned.1.call-update) | async-done | bytes 1048592 | tf_op jit(solution)/shard_map/reduce_scatter | solution.py:17
  71.7 6.5 %gather_fusion = bf16[128,128,256]{2,1,0:T(8,128)(2,1)} fusion(bf16[4,128,256]{2,1,0:T(8,128)(2,1)S(1)} %bitcast.46, s32[1024]{0:T(1024)S(1)} %pad_clamp_fusion), kind=kCustom, calls=%fused_computation | custom fusion | bytes 16777728 | tf_op jit(solution)/shard_map/gather | solution.py:25
  78.1 7.0 %fusion.2 = bf16[32,128,256]{1,2,0:T(8,128)(2,1)S(1)} fusion(bf16[32,4,128,256]{3,2,1,0:T(8,128)(2,1)} %bitcast.48, bf16[32,4,128,128]{3,2,1,0:T(8,128)(2,1)} %param.10), kind=kOutput, calls=%fused_computation.7 | convolution fusion | flops 1074790400 | bytes 14680064 | tf_op jit(solution)/shard_map/skij,skjh->sih/dot_general | solution.py:26
  88.0 4.9 %convolution_convert_fusion.1 = bf16[64,32768]{1,0:T(8,128)(2,1)} fusion(bf16[32,32768]{1,0:T(8,128)(2,1)} %bitcast.51, s32[32]{0:T(128)S(1)} %multiply_add_fusion), kind=kOutput, calls=%fused_computation.2 | convolution fusion | flops 136316928 | bytes 6291584 | tf_op jit(solution)/shard_map/dot_general | solution.py:37
  92.9 7.7 %reshape.74 = bf16[32,2,32768]{2,1,0:T(2,128)(2,1)} reshape(bf16[64,32768]{1,0:T(8,128)(2,1)} %convolution_convert_fusion.1) | data formatting | bytes 8388608 | tf_op jit(solution)/shard_map/reshape | solution.py:40
  100.6 10.5 %all-to-all-start.1 = ((bf16[32,2,32768]{2,1,0:T(2,128)(2,1)}), bf16[32,2,32768]{2,1,0:T(2,128)(2,1)}, u32[]{:S(2)}, u32[]{:S(2)}) async-start(bf16[32,2,32768]{2,1,0:T(2,128)(2,1)} %reshape.74), calls=%async_computation.2 | async-start | bytes 8388608 | tf_op jit(solution)/shard_map/all_to_all | solution.py:44
  112.5 96.4 %all-to-all-done.1 = bf16[32,2,32768]{2,1,0:T(2,128)(2,1)} async-done(((bf16[32,2,32768]{2,1,0:T(2,128)(2,1)}), bf16[32,2,32768]{2,1,0:T(2,128)(2,1)}, u32[]{:S(2)}, u32[]{:S(2)}) %all-to-all-start.1) | async-done | bytes 4194336 | tf_op jit(solution)/shard_map/all_to_all | solution.py:44
  208.9 7.3 %reshape.75 = bf16[64,32768]{1,0:T(8,128)(2,1)} reshape(bf16[32,2,32768]{2,1,0:T(2,128)(2,1)} %all-to-all-done.1) | data formatting | bytes 8388608 | tf_op jit(solution)/shard_map/reshape | solution.py:47
  224.0 7.7 %reshape.78 = bf16[32,2,32768]{2,1,0:T(2,128)(2,1)} reshape(bf16[64,32768]{1,0:T(8,128)(2,1)} %convolution_convert_fusion) | data formatting | bytes 8388608 | tf_op jit(solution)/shard_map/reshape | solution.py:62
  231.7 8.5 %all-to-all-start.2 = ((bf16[32,2,32768]{2,1,0:T(2,128)(2,1)}), bf16[32,2,32768]{2,1,0:T(2,128)(2,1)}, u32[]{:S(2)}, u32[]{:S(2)}) async-start(bf16[32,2,32768]{2,1,0:T(2,128)(2,1)} %reshape.78), calls=%async_computation.3 | async-start | bytes 8388608 | tf_op jit(solution)/shard_map/all_to_all | solution.py:63
  240.5 95.7 %all-to-all-done.2 = bf16[32,2,32768]{2,1,0:T(2,128)(2,1)} async-done(((bf16[32,2,32768]{2,1,0:T(2,128)(2,1)}), bf16[32,2,32768]{2,1,0:T(2,128)(2,1)}, u32[]{:S(2)}, u32[]{:S(2)}) %all-to-all-start.2) | async-done | bytes 4194336 | tf_op jit(solution)/shard_map/all_to_all | solution.py:63
  336.2 7.3 %reshape.79 = bf16[64,32768]{1,0:T(8,128)(2,1)} reshape(bf16[32,2,32768]{2,1,0:T(2,128)(2,1)} %all-to-all-done.2) | data formatting | bytes 8388608 | tf_op jit(solution)/shard_map/reshape | solution.py:63
  347.1 8.1 %fusion = f32[32,256,4,128]{3,1,2,0:T(8,128)} fusion(bf16[32,4,128,128]{3,2,1,0:T(8,128)(2,1)S(1)} %copy-done.1, bf16[32,128,256]{2,1,0:T(8,128)(2,1)S(1)} %bitcast.52), kind=kOutput, calls=%fused_computation.5 | convolution fusion | flops 1073741824 | bytes 23068672 | tf_op jit(solution)/shard_map/skij,sih->skjh/dot_general | solution.py:70
  355.2 17.7 %copy.40 = f32[128,128,256]{2,0,1:T(8,128)} copy(f32[128,128,256]{1,2,0:T(8,128)} %bitcast.47) | data formatting | bytes 33554432 | tf_op jit(solution)/shard_map/reshape | solution.py:74
  372.9 9.0 %convolution_convert_fusion.3 = bf16[4,128,256]{2,0,1:T(4,128)(2,1)S(1)} fusion(f32[128,128,256]{2,0,1:T(8,128)} %copy.40, s32[128]{0:T(128)S(1)} %eq.67), kind=kOutput, calls=%fused_computation.8 | convolution fusion | flops 201458176 | bytes 17039872 | tf_op jit(solution)/shard_map/bn,njh->bjh/dot_general | solution.py:75
  382.8 30.3 %all-gather.2.cloned.1.call-done = bf16[4096,512]{1,0:T(8,128)(2,1)} async-done(((bf16[512,512]{1,0:T(8,128)(2,1)}), bf16[4096,512]{1,0:T(8,128)(2,1)}) %all-gather.2.cloned.1.call-update) | async-done | bytes 4194320 | tf_op jit(solution)/shard_map/all_gather | solution.py:82
  418.2 6.9 %collective-permute-done = f32[128,512]{0,1:T(8,128)S(1)} collective-permute-done((f32[128,512]{0,1:T(8,128)S(1)}, f32[128,512]{0,1:T(8,128)S(1)}, u32[]{:S(2)}, u32[]{:S(2)}) %collective-permute-start) | collective-permute-done | bytes 262176 | tf_op jit(solution)/shard_map/ppermute | solution.py:88
  427.8 11.6 %collective-permute-done.1 = f32[128,512]{0,1:T(8,128)S(1)} collective-permute-done((f32[128,512]{0,1:T(8,128)S(1)}, f32[128,512]{0,1:T(8,128)S(1)}, u32[]{:S(2)}, u32[]{:S(2)}) %collective-permute-start.1) | collective-permute-done | bytes 262176 | tf_op jit(solution)/shard_map/ppermute | solution.py:88
  439.4 5.8 %collective-permute-start.2 = (f32[128,512]{0,1:T(8,128)S(1)}, f32[128,512]{0,1:T(8,128)S(1)}, u32[]{:S(2)}, u32[]{:S(2)}) collective-permute-start(f32[128,512]{0,1:T(8,128)S(1)} %add.72), channel_id=1, source_target_pairs={{0,32},{8,40},{16,48},{24,56},{32,0},{40,8},{48,16},{56,24},{64,96... | collective-permute-start | bytes 786440 | tf_op jit(solution)/shard_map/ppermute | solution.py:88
  445.2 12.1 %collective-permute-done.2 = f32[128,512]{0,1:T(8,128)S(1)} collective-permute-done((f32[128,512]{0,1:T(8,128)S(1)}, f32[128,512]{0,1:T(8,128)S(1)}, u32[]{:S(2)}, u32[]{:S(2)}) %collective-permute-start.2) | collective-permute-done | bytes 262176 | tf_op jit(solution)/shard_map/ppermute | solution.py:88
  458.9 5.2 %collective-permute-done.3 = f32[128,512]{0,1:T(8,128)S(1)} collective-permute-done((f32[128,512]{0,1:T(8,128)S(1)}, f32[128,512]{0,1:T(8,128)S(1)}, u32[]{:S(2)}, u32[]{:S(2)}) %collective-permute-start.3) | collective-permute-done | bytes 262176 | tf_op jit(solution)/shard_map/ppermute | solution.py:88
  468.3 4.4 collective-permute-done.4
  (64 shorter events, 36.5 us)
Async XLA Ops:
  7.2 1.2 copy-start
  7.2 62.3 %reduce-scatter.2.cloned.1.call-start = ((), (), s32[]{:S(2)}) async-start(), calls=%async_computation.4 | async-start | bytes 9437184 | tf_op jit(solution)/shard_map/reduce_scatter | solution.py:17
  13.7 0.7 copy-start.6
  13.7 1.0 copy-start.8
  13.7 13.3 %copy-start.5 = (s32[32,4]{0,1:T(4,128)S(1)}, s32[32,4]{0,1:T(4,128)}, u32[]{:S(2)}) copy-start(s32[32,4]{0,1:T(4,128)} %param.13) | copy-start | bytes 1540
  15.6 85.1 %all-to-all-start = ((s32[32,1,2]{2,1,0:T(1,128)}), s32[32,1,2]{2,1,0:T(1,128)S(1)}, u32[]{:S(2)}, u32[]{:S(2)}) async-start(s32[32,1,2]{2,1,0:T(1,128)} %bitcast.2), calls=%async_computation | async-start | bytes 32768 | tf_op jit(solution)/shard_map/all_to_all | solution.py:45
  70.8 0.8 copy-start.2
  100.6 10.5 %copy-start.7 = (s32[512]{0:T(512)S(1)}, s32[512]{0:T(512)}, u32[]{:S(2)}) copy-start(s32[512]{0:T(512)} %param.14) | copy-start | bytes 6148
  100.6 108.3 %all-to-all-start.1 = ((bf16[32,2,32768]{2,1,0:T(2,128)(2,1)}), bf16[32,2,32768]{2,1,0:T(2,128)(2,1)}, u32[]{:S(2)}, u32[]{:S(2)}) async-start(bf16[32,2,32768]{2,1,0:T(2,128)(2,1)} %reshape.74), calls=%async_computation.2 | async-start | bytes 8388608 | tf_op jit(solution)/shard_map/all_to_all | solution.py:44
  216.2 3.3 copy-start.3
  216.2 3.3 copy-start.4
  231.7 104.5 %all-to-all-start.2 = ((bf16[32,2,32768]{2,1,0:T(2,128)(2,1)}), bf16[32,2,32768]{2,1,0:T(2,128)(2,1)}, u32[]{:S(2)}, u32[]{:S(2)}) async-start(bf16[32,2,32768]{2,1,0:T(2,128)(2,1)} %reshape.78), calls=%async_computation.3 | async-start | bytes 8388608 | tf_op jit(solution)/shard_map/all_to_all | solution.py:63
  240.2 172.9 %all-gather.2.cloned.1.call-start = ((), (), s32[]{:S(2)}) async-start(), calls=%async_computation.5 | async-start | bytes 4718592 | tf_op jit(solution)/shard_map/all_gather | solution.py:82
  343.5 3.6 copy-start.1
  416.6 8.5 %collective-permute-start = (f32[128,512]{0,1:T(8,128)S(1)}, f32[128,512]{0,1:T(8,128)S(1)}, u32[]{:S(2)}, u32[]{:S(2)}) collective-permute-start(f32[128,512]{0,1:T(8,128)S(1)} %convolution_bitcast_fusion), channel_id=1, source_target_pairs={{0,8},{8,0},{16,24},{24,16},{32,40},{40,32},{48,56},{56,48},{64,72... | collective-permute-start | bytes 786440 | tf_op jit(solution)/shard_map/ppermute | solution.py:88
  425.1 14.2 %collective-permute-start.1 = (f32[128,512]{0,1:T(8,128)S(1)}, f32[128,512]{0,1:T(8,128)S(1)}, u32[]{:S(2)}, u32[]{:S(2)}) collective-permute-start(f32[128,512]{0,1:T(8,128)S(1)} %add.71), channel_id=1, source_target_pairs={{0,16},{8,24},{16,0},{24,8},{32,48},{40,56},{48,32},{56,40},{64,80... | collective-permute-start | bytes 786440 | tf_op jit(solution)/shard_map/ppermute | solution.py:88
  439.4 17.9 %collective-permute-start.2 = (f32[128,512]{0,1:T(8,128)S(1)}, f32[128,512]{0,1:T(8,128)S(1)}, u32[]{:S(2)}, u32[]{:S(2)}) collective-permute-start(f32[128,512]{0,1:T(8,128)S(1)} %add.72), channel_id=1, source_target_pairs={{0,32},{8,40},{16,48},{24,56},{32,0},{40,8},{48,16},{56,24},{64,96... | collective-permute-start | bytes 786440 | tf_op jit(solution)/shard_map/ppermute | solution.py:88
  457.3 6.8 %collective-permute-start.3 = (f32[128,512]{0,1:T(8,128)S(1)}, f32[128,512]{0,1:T(8,128)S(1)}, u32[]{:S(2)}, u32[]{:S(2)}) collective-permute-start(f32[128,512]{0,1:T(8,128)S(1)} %add.73), channel_id=1, source_target_pairs={{0,64},{8,72},{16,80},{24,88},{32,96},{40,104},{48,112},{56,120},{... | collective-permute-start | bytes 786440 | tf_op jit(solution)/shard_map/ppermute | solution.py:88
  464.2 8.5 %collective-permute-start.4 = (f32[128,512]{0,1:T(8,128)S(1)}, f32[128,512]{0,1:T(8,128)S(1)}, u32[]{:S(2)}, u32[]{:S(2)}) collective-permute-start(f32[128,512]{0,1:T(8,128)S(1)} %add.74), channel_id=1, source_target_pairs={{0,128},{8,136},{16,144},{24,152},{32,160},{40,168},{48,176},{56,1... | collective-permute-start | bytes 786440 | tf_op jit(solution)/shard_map/ppermute | solution.py:88
Sparse Core Ops, SparseCore 0:
  13.9 55.5 reduce-scatter.1
  382.9 30.1 all-gather.1
